TPU v7x, 32 devices: a whole 2x2x4 slice. The times are simulated.
32 devices in a mesh: ctx: 8 (over z, y), tp: 4 (over x, core).
Axes of the slice: x: 2, y: 2, z: 4, core: 2. Of those that a mesh axis runs over, the one named last changes fastest.
Arguments:
- qkv: bfloat16 [1024, 3, 8192], P(('ctx', 'tp')), may hold values from -6 to 6
- filters: float32 [3, 7, 8192], P(None, None, 'tp'), may hold values from -1.5 to 1.5
- doc_ids: int32 [8], replicated, may hold values from 0 to 1, never falling along the last dimension, each value on 1 to 5 neighbouring positions
- upstream: bfloat16 [1024, 8192], P('ctx', 'tp'), may hold values from -6 to 6
Outputs:
- attended: bfloat16 [1024, 8192], P('ctx', 'tp')
- qkv_grad: bfloat16 [1024, 3, 8192], P(('ctx', 'tp'))
- filter_grad: float32 [3, 7, 8192], P(None, None, 'tp')
Inputs may be any that keep to these rules, and one draw needn't show every extreme that they name: doc_ids never falls along the sequence; every document covers 1 to 5 whole blocks of 128 tokens.
All inputs are finite; a program needn't handle non-finite values.
Results may differ from a plain program's by a relative error of at most 0.014.
The roundings to bfloat16 on the way count: a program that leaves them out, or rounds other values in their place, can miss the bound.
Values may be sent and summed in bfloat16 or wider, within the bound.
No kernel may reach another device: no remote copies, remote signals or barrier semaphores. Data moves between devices by JAX's collectives and lax.ppermute only.
A program may use at most 128 MiB of HBM per device.

v0:
```python
import jax
import jax.numpy as jnp
from jax import lax
from jax.sharding import PartitionSpec as P

HEAD_DIM = 128
KW = 7
BLOCK = 128
STEPS = 4


def from_behind(value, axis, steps):
    count = lax.axis_size(axis)
    first, last = (max(0, -steps), min(count, count - steps))
    return lax.ppermute(value, axis, [(source, source + steps) for source in range(first, last)])


def block_docs(doc_ids, first_block, count):
    start = jnp.maximum(first_block, 0)
    picked = lax.dynamic_slice_in_dim(doc_ids, start, count)
    return jnp.repeat(picked, BLOCK)


def shards(qkv, filters, doc_ids, upstream):
    local = lax.all_to_all(qkv, "tp", split_axis=2, concat_axis=0, tiled=True)
    tokens = local.shape[0]
    width = local.shape[2]
    heads = width // HEAD_DIM
    blocks_here = tokens // BLOCK
    logit_scale = HEAD_DIM ** (-0.5)
    position = lax.axis_index("ctx")
    reach = STEPS + 1
    rim = from_behind(local[tokens - (KW - 1) :], "ctx", 1)
    inputs = jnp.concatenate([rim, local], axis=0).astype(jnp.float32)
    mixed = sum(
        (filters[:, lag, :] * inputs[KW - 1 - lag : KW - 1 - lag + tokens] for lag in range(KW))
    )
    mixed = mixed.astype(jnp.bfloat16)
    queries = mixed[:, 0].reshape(tokens, heads, HEAD_DIM)
    key_value = mixed[:, 1:3]
    tiles = [key_value]
    current = key_value
    for distance in range(1, STEPS + 1):
        current = from_behind(current, "ctx", 1)
        tiles.append(current)
    joined = jnp.concatenate(tiles, axis=0)
    keys = joined[:, 0].reshape(reach * tokens, heads, HEAD_DIM)
    values = joined[:, 1].reshape(reach * tokens, heads, HEAD_DIM)
    rows = jnp.arange(tokens)
    query_token = position * tokens + rows
    query_doc = block_docs(doc_ids, position * blocks_here, blocks_here)
    key_tokens = jnp.concatenate(
        [(position - distance) * tokens + rows for distance in range(reach)]
    )
    key_docs = jnp.concatenate(
        [
            block_docs(doc_ids, (position - distance) * blocks_here, blocks_here)
            for distance in range(reach)
        ]
    )
    allowed = (
        (key_tokens[None, :] >= 0)
        & (key_tokens[None, :] <= query_token[:, None])
        & (key_docs[None, :] == query_doc[:, None])
    )
    raw = (
        jnp.einsum("qhd,khd->hqk", queries, keys, preferred_element_type=jnp.float32) * logit_scale
    )
    masked = jnp.where(allowed[None], raw, -1e30)
    row_max = masked.max(axis=2)
    expo = jnp.where(allowed[None], jnp.exp(masked - row_max[:, :, None]), 0.0)
    row_sum = expo.sum(axis=2)
    weighted_values = jnp.einsum(
        "hqk,khd->qhd", expo.astype(jnp.bfloat16), values, preferred_element_type=jnp.float32
    )
    attended = (weighted_values / row_sum.T[:, :, None]).astype(jnp.bfloat16)
    grad_out = upstream.reshape(tokens, heads, HEAD_DIM)
    delta = jnp.sum(grad_out.astype(jnp.float32) * attended.astype(jnp.float32), axis=-1).T
    prob = expo / row_sum[:, :, None]
    value_part = jnp.einsum(
        "hqk,qhd->khd", prob.astype(jnp.bfloat16), grad_out, preferred_element_type=jnp.float32
    )
    probability_gradient = jnp.einsum(
        "qhd,khd->hqk", grad_out, values, preferred_element_type=jnp.float32
    )
    score_gradient = (prob * (probability_gradient - delta[:, :, None]) * logit_scale).astype(
        jnp.bfloat16
    )
    query_gradient_rows = jnp.einsum(
        "hqk,khd->qhd", score_gradient, keys, preferred_element_type=jnp.float32
    )
    key_part = jnp.einsum(
        "hqk,qhd->khd", score_gradient, queries, preferred_element_type=jnp.float32
    )
    stacked = jnp.stack(
        [key_part.reshape(reach, tokens, width), value_part.reshape(reach, tokens, width)], axis=2
    )
    partials = [stacked[distance] for distance in range(reach)]
    carried = partials[STEPS]
    for distance in range(STEPS - 1, -1, -1):
        carried = from_behind(carried, "ctx", -1)
        carried = carried + partials[distance]
    conv_grad = jnp.concatenate([query_gradient_rows.reshape(tokens, 1, width), carried], axis=1)
    grad_edge = from_behind(conv_grad[: KW - 1], "ctx", -1)
    extended = jnp.concatenate([conv_grad, grad_edge], axis=0)
    input_grad = sum((filters[:, lag, :] * extended[lag : lag + tokens] for lag in range(KW)))
    tap_terms = jnp.stack(
        [
            jnp.sum(inputs[KW - 1 - lag : KW - 1 - lag + tokens] * conv_grad, axis=0)
            for lag in range(KW)
        ],
        axis=1,
    )
    filter_grad = lax.psum(tap_terms, "ctx")
    qkv_grad = lax.all_to_all(
        input_grad.astype(jnp.bfloat16), "tp", split_axis=0, concat_axis=2, tiled=True
    )
    return (attended.reshape(tokens, width), qkv_grad, filter_grad)


def solution(mesh):
    return jax.shard_map(
        shards,
        mesh=mesh,
        in_specs=(P(("ctx", "tp"), None, None), P(None, None, "tp"), P(), P("ctx", "tp")),
        out_specs=(P("ctx", "tp"), P(("ctx", "tp"), None, None), P(None, None, "tp")),
        check_vma=False,
    )
```

profile of v0, /device:TPU:0, one launch (start us, length us, event | category | flops | bytes accessed | tf_op | source)
XLA Modules:
  0.0 541.6 jit_solution(776772498163065581)
XLA Ops:
  7.2 10.7 %copy.57 = bf16[32,3,8192]{0,1,2:T(4,128)(2,1)} copy(bf16[32,3,8192]{2,0,1:T(8,128)(2,1)} %param.4) | data formatting | bytes 3145728 | tf_op args[0]
  17.8 8.4 %reshape.158 = bf16[4,2,98304]{2,1,0:T(2,128)(2,1)} reshape(bf16[8192,3,32]{2,1,0:T(4,128)(2,1)} %bitcast.114) | data formatting | bytes 3145728
  26.2 4.3 all-to-all-start
  30.7 19.9 %all-to-all-done = bf16[4,2,98304]{2,1,0:T(2,128)(2,1)S(1)} async-done(((bf16[4,2,98304]{2,1,0:T(2,128)(2,1)}), bf16[4,2,98304]{2,1,0:T(2,128)(2,1)S(1)}, u32[]{:S(2)}, u32[]{:S(2)}) %all-to-all-start) | async-done | bytes 1572896 | tf_op jit(solution)/shard_map/all_to_all | solution.py:25
  50.6 7.1 %reshape.159 = bf16[8192,3,32]{2,1,0:T(4,128)(2,1)} reshape(bf16[4,2,98304]{2,1,0:T(2,128)(2,1)S(1)} %all-to-all-done) | data formatting | bytes 3145728
  57.7 10.5 %copy.59 = bf16[4,32,3,2048]{3,1,0,2:T(8,128)(2,1)S(1)} copy(bf16[4,32,3,2048]{1,2,3,0:T(4,128)(2,1)} %bitcast.113) | data formatting | bytes 3145728 | tf_op jit(solution)/shard_map/all_to_all | solution.py:25
  68.2 4.2 collective-permute-start
  81.5 5.3 collective-permute-start.1
  86.8 20.0 %collective-permute-done.1 = bf16[128,2,2048]{2,0,1:T(8,128)(2,1)} collective-permute-done((bf16[128,2,2048]{2,0,1:T(8,128)(2,1)S(1)}, bf16[128,2,2048]{2,0,1:T(8,128)(2,1)}, u32[]{:S(2)}, u32[]{:S(2)}) %collective-permute-start.1) | collective-permute-done | bytes 1048608 | tf_op jit(solution)/shard_map/ppermute | solution.py:15
  106.8 5.5 %collective-permute-start.2 = (bf16[128,2,2048]{2,0,1:T(8,128)(2,1)}, bf16[128,2,2048]{2,0,1:T(8,128)(2,1)}, u32[]{:S(2)}, u32[]{:S(2)}) collective-permute-start(bf16[128,2,2048]{2,0,1:T(8,128)(2,1)} %collective-permute-done.1), channel_id=1, source_target_pairs={{0,4},{4,8},{8,12},{12,16},{16,20},{20,24},{24,28},{1,5},{5,9},{9,... | collective-permute-start | bytes 3145736 | tf_op jit(solution)/shard_map/ppermute | solution.py:15
  112.8 19.0 %collective-permute-done.2 = bf16[128,2,2048]{2,0,1:T(8,128)(2,1)} collective-permute-done((bf16[128,2,2048]{2,0,1:T(8,128)(2,1)}, bf16[128,2,2048]{2,0,1:T(8,128)(2,1)}, u32[]{:S(2)}, u32[]{:S(2)}) %collective-permute-start.2) | collective-permute-done | bytes 1048608 | tf_op jit(solution)/shard_map/ppermute | solution.py:15
  131.8 6.2 %collective-permute-start.3 = (bf16[128,2,2048]{2,0,1:T(8,128)(2,1)}, bf16[128,2,2048]{2,0,1:T(8,128)(2,1)}, u32[]{:S(2)}, u32[]{:S(2)}) collective-permute-start(bf16[128,2,2048]{2,0,1:T(8,128)(2,1)} %collective-permute-done.2), channel_id=1, source_target_pairs={{0,4},{4,8},{8,12},{12,16},{16,20},{20,24},{24,28},{1,5},{5,9},{9,... | collective-permute-start | bytes 3145736 | tf_op jit(solution)/shard_map/ppermute | solution.py:15
  141.8 14.7 %collective-permute-done.3 = bf16[128,2,2048]{2,0,1:T(8,128)(2,1)} collective-permute-done((bf16[128,2,2048]{2,0,1:T(8,128)(2,1)}, bf16[128,2,2048]{2,0,1:T(8,128)(2,1)}, u32[]{:S(2)}, u32[]{:S(2)}) %collective-permute-start.3) | collective-permute-done | bytes 1048608 | tf_op jit(solution)/shard_map/ppermute | solution.py:15
  156.5 6.3 %collective-permute-start.4 = (bf16[128,2,2048]{2,0,1:T(8,128)(2,1)}, bf16[128,2,2048]{2,0,1:T(8,128)(2,1)}, u32[]{:S(2)}, u32[]{:S(2)}) collective-permute-start(bf16[128,2,2048]{2,0,1:T(8,128)(2,1)} %collective-permute-done.3), channel_id=1, source_target_pairs={{0,4},{4,8},{8,12},{12,16},{16,20},{20,24},{24,28},{1,5},{5,9},{9,... | collective-permute-start | bytes 3145736 | tf_op jit(solution)/shard_map/ppermute | solution.py:15
  182.7 5.7 %fusion.48 = (bf16[640,1,2048]{2,0,1:T(8,128)(2,1)}, bf16[640,1,2048]{2,0,1:T(8,128)(2,1)}) fusion(bf16[640,2,2048]{2,0,1:T(8,128)(2,1)} %constant_dynamic-update-slice_fusion), kind=kLoop, calls=%fused_computation.106 | loop fusion | bytes 10485760 | tf_op jit(solution)/shard_map/slice | solution.py:47
  188.4 4.4 copy.62
  192.8 4.5 copy.60
  197.2 6.6 %fusion.52 = (f32[16,128]{1,0:T(8,128)S(1)}, f32[16,128,640]{2,1,0:T(8,128)}) fusion(pred[128,640]{1,0:T(8,128)(4,1)} %and_and_fusion, bf16[128,16,128]{0,2,1:T(8,128)(2,1)} %bitcast.124, bf16[640,16,128]{0,2,1:T(8,128)(2,1)} %bitcast.115), kind=kOutput, calls=%fused_computation.110 | convolution fusion | flops 342098560 | bytes 8478720 | tf_op jit(solution)/shard_map/sub | solution.py:71
  203.8 4.1 fusion.18
  213.3 5.3 copy.72
  218.6 6.8 %stack_reshape.7 = f32[5,128,1,2048]{3,1,0,2:T(8,128)} reshape(f32[640,16,128]{2,1,0:T(8,128)} %copy.72) | data formatting | bytes 10485760 | tf_op jit(solution)/shard_map/stack;reshape | solution.py:95
  225.4 5.0 convolution_bitcast_fusion
  230.5 7.4 %reshape.152 = f32[5,128,1,2048]{1,0,3,2:T(8,128)} reshape(f32[640,16,128]{0,2,1:T(8,128)} %convolution_bitcast_fusion) | data formatting | bytes 10485760 | tf_op jit(solution)/shard_map/stack;reshape | solution.py:95
  237.8 7.9 %copy.73 = f32[5,128,1,2048]{3,1,2,0:T(8,128)} copy(f32[5,128,1,2048]{1,0,3,2:T(8,128)} %reshape.152) | data formatting | bytes 10485760 | tf_op jit(solution)/shard_map/stack;reshape | solution.py:95
  249.1 44.7 %collective-permute-done.5 = f32[128,2,2048]{2,0,1:T(8,128)S(1)} collective-permute-done((f32[128,2,2048]{2,0,1:T(8,128)S(1)}, f32[128,2,2048]{2,0,1:T(8,128)S(1)}, u32[]{:S(2)}, u32[]{:S(2)}) %collective-permute-start.5) | collective-permute-done | bytes 2097184 | tf_op jit(solution)/shard_map/ppermute | solution.py:15
  295.7 44.1 %collective-permute-done.6 = f32[128,2,2048]{2,0,1:T(8,128)S(1)} collective-permute-done((f32[128,2,2048]{2,0,1:T(8,128)S(1)}, f32[128,2,2048]{2,0,1:T(8,128)S(1)}, u32[]{:S(2)}, u32[]{:S(2)}) %collective-permute-start.6) | collective-permute-done | bytes 2097184 | tf_op jit(solution)/shard_map/ppermute | solution.py:15
  341.7 42.9 %collective-permute-done.7 = f32[128,2,2048]{2,0,1:T(8,128)S(1)} collective-permute-done((f32[128,2,2048]{2,0,1:T(8,128)S(1)}, f32[128,2,2048]{2,0,1:T(8,128)S(1)}, u32[]{:S(2)}, u32[]{:S(2)}) %collective-permute-start.7) | collective-permute-done | bytes 2097184 | tf_op jit(solution)/shard_map/ppermute | solution.py:15
  392.0 37.3 %collective-permute-done.8 = f32[128,2,2048]{2,0,1:T(8,128)} collective-permute-done((f32[128,2,2048]{2,0,1:T(8,128)}, f32[128,2,2048]{2,0,1:T(8,128)}, u32[]{:S(2)}, u32[]{:S(2)}) %collective-permute-start.8) | collective-permute-done | bytes 2097184 | tf_op jit(solution)/shard_map/ppermute | solution.py:15
  431.9 3.6 multiply_reduce_fusion
  437.5 6.2 %collective-permute-done.9 = f32[6,3,2048]{2,0,1:T(8,128)S(1)} collective-permute-done((f32[6,3,2048]{2,0,1:T(8,128)S(1)}, f32[6,3,2048]{2,0,1:T(8,128)S(1)}, u32[]{:S(2)}, u32[]{:S(2)}) %collective-permute-start.9) | collective-permute-done | bytes 147488 | tf_op jit(solution)/shard_map/ppermute | solution.py:15
  449.5 3.7 all-to-all-start.1
  456.3 74.4 %all-reduce.2.cloned.1.call-done = f32[3,7,2048]{2,0,1:T(4,128)} async-done(((f32[3,7,2048]{2,0,1:T(4,128)}), f32[3,7,2048]{2,0,1:T(4,128)}) %all-reduce.2.cloned.1.call-update) | async-done | bytes 172048 | tf_op jit(solution)/shard_map/psum | solution.py:114
  (107 shorter events, 70.5 us)
Async XLA Ops:
  26.2 4.3 copy-start.13
  26.2 24.4 %all-to-all-start = ((bf16[4,2,98304]{2,1,0:T(2,128)(2,1)}), bf16[4,2,98304]{2,1,0:T(2,128)(2,1)S(1)}, u32[]{:S(2)}, u32[]{:S(2)}) async-start(bf16[4,2,98304]{2,1,0:T(2,128)(2,1)} %reshape.158), calls=%async_computation | async-start | bytes 3145728 | tf_op jit(solution)/shard_map/all_to_all | solution.py:25
  68.2 4.3 copy-start.5
  68.2 6.4 %collective-permute-start = (bf16[6,3,2048]{2,0,1:T(8,128)(2,1)S(1)}, bf16[6,3,2048]{2,0,1:T(8,128)(2,1)S(1)}, u32[]{:S(2)}, u32[]{:S(2)}) collective-permute-start(bf16[6,3,2048]{2,0,1:T(8,128)(2,1)S(1)} %slice.138), channel_id=1, source_target_pairs={{0,4},{4,8},{8,12},{12,16},{16,20},{20,24},{24,28},{1,5},{5,9},{9,... | collective-permute-start | bytes 221192 | tf_op jit(solution)/shard_map/ppermute | solution.py:15
  72.5 6.7 %copy-start.11 = (f32[3,1,2048]{2,0,1:T(4,128)}, f32[3,1,2048]{2,0,1:T(4,128)S(1)}, u32[]{:S(2)}) copy-start(f32[3,1,2048]{2,0,1:T(4,128)S(1)} %copy.107) | copy-start | bytes 73732
  79.2 1.1 copy-start.6
  80.4 57.7 %copy-start.17 = (s32[8]{0:T(128)S(1)}, s32[8]{0:T(128)}, u32[]{:S(2)}) copy-start(s32[8]{0:T(128)} %param.6) | copy-start | bytes 100
  81.5 25.4 %collective-permute-start.1 = (bf16[128,2,2048]{2,0,1:T(8,128)(2,1)S(1)}, bf16[128,2,2048]{2,0,1:T(8,128)(2,1)}, u32[]{:S(2)}, u32[]{:S(2)}) collective-permute-start(bf16[128,2,2048]{2,0,1:T(8,128)(2,1)S(1)} %get-tuple-element.24), channel_id=1, source_target_pairs={{0,4},{4,8},{8,12},{12,16},{16,20},{20,24},{24,28},{1,5},{5,9},{9,... | collective-permute-start | bytes 3145736 | tf_op jit(solution)/shard_map/ppermute | solution.py:15
  106.8 24.9 %collective-permute-start.2 = (bf16[128,2,2048]{2,0,1:T(8,128)(2,1)}, bf16[128,2,2048]{2,0,1:T(8,128)(2,1)}, u32[]{:S(2)}, u32[]{:S(2)}) collective-permute-start(bf16[128,2,2048]{2,0,1:T(8,128)(2,1)} %collective-permute-done.1), channel_id=1, source_target_pairs={{0,4},{4,8},{8,12},{12,16},{16,20},{20,24},{24,28},{1,5},{5,9},{9,... | collective-permute-start | bytes 3145736 | tf_op jit(solution)/shard_map/ppermute | solution.py:15
  131.8 24.7 %collective-permute-start.3 = (bf16[128,2,2048]{2,0,1:T(8,128)(2,1)}, bf16[128,2,2048]{2,0,1:T(8,128)(2,1)}, u32[]{:S(2)}, u32[]{:S(2)}) collective-permute-start(bf16[128,2,2048]{2,0,1:T(8,128)(2,1)} %collective-permute-done.2), channel_id=1, source_target_pairs={{0,4},{4,8},{8,12},{12,16},{16,20},{20,24},{24,28},{1,5},{5,9},{9,... | collective-permute-start | bytes 3145736 | tf_op jit(solution)/shard_map/ppermute | solution.py:15
  156.5 23.9 %collective-permute-start.4 = (bf16[128,2,2048]{2,0,1:T(8,128)(2,1)}, bf16[128,2,2048]{2,0,1:T(8,128)(2,1)}, u32[]{:S(2)}, u32[]{:S(2)}) collective-permute-start(bf16[128,2,2048]{2,0,1:T(8,128)(2,1)} %collective-permute-done.3), channel_id=1, source_target_pairs={{0,4},{4,8},{8,12},{12,16},{16,20},{20,24},{24,28},{1,5},{5,9},{9,... | collective-permute-start | bytes 3145736 | tf_op jit(solution)/shard_map/ppermute | solution.py:15
  203.8 4.1 copy-start.4
  203.8 5.0 copy-start.7
  203.8 5.0 copy-start.9
  245.7 48.1 %slice-start = ((s8[5242880]{0:T(1024)(128)(4,1)}), s8[4194304]{0:T(1024)(128)(4,1)S(1)}, s32[]{:S(2)}) async-start(s8[5242880]{0:T(1024)(128)(4,1)} %bitcast.108), calls=%async_computation.3 | async-start | bytes 8388608
  245.7 48.1 %slice-start.1 = ((s8[5242880]{0:T(1024)(128)(4,1)}), s8[1048576]{0:T(1024)(128)(4,1)S(1)}, s32[]{:S(2)}) async-start(s8[5242880]{0:T(1024)(128)(4,1)} %bitcast.108), calls=%async_computation.4 | async-start | bytes 2097152
  245.7 48.1 %copy-start = (f32[5,128,1,2048]{3,1,2,0:T(8,128)S(1)}, f32[5,128,1,2048]{3,1,2,0:T(8,128)}, u32[]{:S(2)}) copy-start(f32[5,128,1,2048]{3,1,2,0:T(8,128)} %copy.73) | copy-start | bytes 15728644
  247.5 46.3 %collective-permute-start.5 = (f32[128,2,2048]{2,0,1:T(8,128)S(1)}, f32[128,2,2048]{2,0,1:T(8,128)S(1)}, u32[]{:S(2)}, u32[]{:S(2)}) collective-permute-start(f32[128,2,2048]{2,0,1:T(8,128)S(1)} %fusion.25), channel_id=1, source_target_pairs={{4,0},{8,4},{12,8},{16,12},{20,16},{24,20},{28,24},{5,1},{9,5},{13... | collective-permute-start | bytes 6291464 | tf_op jit(solution)/shard_map/ppermute | solution.py:15
  294.2 45.6 %collective-permute-start.6 = (f32[128,2,2048]{2,0,1:T(8,128)S(1)}, f32[128,2,2048]{2,0,1:T(8,128)S(1)}, u32[]{:S(2)}, u32[]{:S(2)}) collective-permute-start(f32[128,2,2048]{2,0,1:T(8,128)S(1)} %fusion.28), channel_id=1, source_target_pairs={{4,0},{8,4},{12,8},{16,12},{20,16},{24,20},{28,24},{5,1},{9,5},{13... | collective-permute-start | bytes 6291464 | tf_op jit(solution)/shard_map/ppermute | solution.py:15
  340.1 47.3 %copy-start.2 = (bf16[640,1,2048]{0,2,1:T(8,128)(2,1)S(1)}, bf16[640,1,2048]{0,2,1:T(8,128)(2,1)}, u32[]{:S(2)}) copy-start(bf16[640,1,2048]{0,2,1:T(8,128)(2,1)} %copy.62) | copy-start | bytes 7864324
  340.1 47.3 %copy-start.3 = (bf16[16,128,640]{2,1,0:T(8,128)(2,1)S(1)}, bf16[16,128,640]{2,1,0:T(8,128)(2,1)}, u32[]{:S(2)}) copy-start(bf16[16,128,640]{2,1,0:T(8,128)(2,1)} %fusion.2) | copy-start | bytes 7864324
  340.1 44.4 %collective-permute-start.7 = (f32[128,2,2048]{2,0,1:T(8,128)S(1)}, f32[128,2,2048]{2,0,1:T(8,128)S(1)}, u32[]{:S(2)}, u32[]{:S(2)}) collective-permute-start(f32[128,2,2048]{2,0,1:T(8,128)S(1)} %fusion.31), channel_id=1, source_target_pairs={{4,0},{8,4},{12,8},{16,12},{20,16},{24,20},{28,24},{5,1},{9,5},{13... | collective-permute-start | bytes 6291464 | tf_op jit(solution)/shard_map/ppermute | solution.py:15
  386.1 43.2 %collective-permute-start.8 = (f32[128,2,2048]{2,0,1:T(8,128)}, f32[128,2,2048]{2,0,1:T(8,128)}, u32[]{:S(2)}, u32[]{:S(2)}) collective-permute-start(f32[128,2,2048]{2,0,1:T(8,128)} %fusion.23), channel_id=1, source_target_pairs={{4,0},{8,4},{12,8},{16,12},{20,16},{24,20},{28,24},{5,1},{9,5},{13... | collective-permute-start | bytes 6291464 | tf_op jit(solution)/shard_map/ppermute | solution.py:15
  392.0 39.8 %copy-start.1 = (f32[128,1,2048]{2,0,1:T(8,128)S(1)}, f32[128,1,2048]{2,0,1:T(8,128)}, u32[]{:S(2)}) copy-start(f32[128,1,2048]{2,0,1:T(8,128)} %copy.75) | copy-start | bytes 3145732
  435.5 8.3 %collective-permute-start.9 = (f32[6,3,2048]{2,0,1:T(8,128)S(1)}, f32[6,3,2048]{2,0,1:T(8,128)S(1)}, u32[]{:S(2)}, u32[]{:S(2)}) collective-permute-start(f32[6,3,2048]{2,0,1:T(8,128)S(1)} %fusion.45), channel_id=1, source_target_pairs={{4,0},{8,4},{12,8},{16,12},{20,16},{24,20},{28,24},{5,1},{9,5},{13... | collective-permute-start | bytes 442376 | tf_op jit(solution)/shard_map/ppermute | solution.py:15
  437.5 6.6 %copy-start.12 = (f32[3,1,2048]{2,0,1:T(4,128)S(1)}, f32[3,1,2048]{2,0,1:T(4,128)}, u32[]{:S(2)}) copy-start(f32[3,1,2048]{2,0,1:T(4,128)} %copy-done.11) | copy-start | bytes 73732
  446.8 6.5 %copy-start.16 = (f32[3,2048]{1,0:T(4,128)S(1)}, f32[3,2048]{1,0:T(4,128)}, u32[]{:S(2)}) copy-start(f32[3,2048]{1,0:T(4,128)} %get-tuple-element.17) | copy-start | bytes 73732
  446.8 7.2 %copy-start.15 = (f32[3,2048]{1,0:T(4,128)S(1)}, f32[3,2048]{1,0:T(4,128)}, u32[]{:S(2)}) copy-start(f32[3,2048]{1,0:T(4,128)} %get-tuple-element.16) | copy-start | bytes 73732
  446.8 7.8 %copy-start.14 = (f32[3,2048]{1,0:T(4,128)S(1)}, f32[3,2048]{1,0:T(4,128)}, u32[]{:S(2)}) copy-start(f32[3,2048]{1,0:T(4,128)} %get-tuple-element.15) | copy-start | bytes 73732
  449.5 5.7 %copy-start.8 = (bf16[128,16,128]{0,2,1:T(8,128)(2,1)S(1)}, bf16[128,16,128]{0,2,1:T(8,128)(2,1)}, u32[]{:S(2)}) copy-start(bf16[128,16,128]{0,2,1:T(8,128)(2,1)} %get-tuple-element.41) | copy-start | bytes 1572868
  449.5 82.8 %all-to-all-start.1 = ((bf16[128,3,2048]{2,1,0:T(4,128)(2,1)}), bf16[128,3,2048]{2,1,0:T(4,128)(2,1)S(1)}, u32[]{:S(2)}, u32[]{:S(2)}) async-start(bf16[128,3,2048]{2,1,0:T(4,128)(2,1)} %copy.76), calls=%async_computation.1 | async-start | bytes 4194304 | tf_op jit(solution)/shard_map/all_to_all | solution.py:115
  453.3 77.4 %all-reduce.2.cloned.1.call-start = ((), (), s32[]{:S(2)}) async-start(), calls=%async_computation.2 | async-start | bytes 458752 | tf_op jit(solution)/shard_map/psum | solution.py:114
  (1 other events, 0.7 us)
Sparse Core Ops, SparseCore 0:
  458.1 72.5 all-reduce.1
where the time goes:
time: 544 us; the launch traced here: 542 us
  waiting for transfers between devices  328 us (60%)
  local copies, waits for them, and re-layouts  114 us (21%)
  starting transfers between devices  42.9 us (8%)
  matrix products  22.2 us (4%)
  other arithmetic  20.2 us (4%)
  between operations  14.5 us (3%)
    ppermute x10, waiting for transfers between devices, from_behind(): lax.ppermute(value, axis, [(source, source + steps) for source in range(f...  234 us
    psum x1, waiting for transfers between devices, shards(): filter_grad = lax.psum(tap_terms, 'ctx')  74.4 us
    unnamed x63, local copies, waits for them, and re-layouts  44.5 us
    ppermute x10, starting transfers between devices, from_behind(): lax.ppermute(value, axis, [(source, source + steps) for source in range(f...  34.8 us
    another operation x3, local copies, waits for them, and re-layouts, shards(): jnp.stack([key_part.reshape(reach, tokens, width), value_part.reshape(rea...  22 us
    all_to_all x1, waiting for transfers between devices, shards(): local = lax.all_to_all(qkv, 'tp', split_axis=2, concat_axis=0, tiled=True)  19.9 us
  transfers between devices with their start and end apart: 13, of which 12 were waited for; matrix products, arithmetic and copies ran while one was open for 5% of the time, Pallas kernels for 0%

commit v1 on v0

--- a/solution.py
+++ b/solution.py
@@ -111,7 +111,7 @@
         ],
         axis=1,
     )
-    filter_grad = lax.psum(tap_terms, "ctx")
+    filter_grad = jnp.sum(lax.all_gather(tap_terms, "ctx"), axis=0)
     qkv_grad = lax.all_to_all(
         input_grad.astype(jnp.bfloat16), "tp", split_axis=0, concat_axis=2, tiled=True
     )

time: 544 us -> 498 us (0.915)
  waiting for transfers between devices: 328 us -> 282 us
    psum x1 -> x0, waiting for transfers between devices: 74.4 us -> none  [shards(): filter_grad = lax.psum(tap_terms, 'ctx')]
    all_to_all x1, waiting for transfers between devices: 0.01 us -> 24.6 us  [shards(): lax.all_to_all(input_grad.astype(jnp.bfloat16), 'tp', split_axis=0, conca...]
    all_gather x0 -> x1, waiting for transfers between devices: none -> 6.76 us  [shards(): filter_grad = jnp.sum(lax.all_gather(tap_terms, 'ctx'), axis=0)]
    unnamed x63 -> x54, local copies, waits for them, and re-layouts: 44.5 us -> 40.7 us
  transfers between devices with their start and end apart: 13 -> 13, of which waited for: 12 -> 13; matrix products, arithmetic and copies ran while one was open for 5% -> 8% of each run, Pallas kernels for 0% -> 0%
where the time goes in v1:
time: 498 us; the launch traced here: 496 us
  waiting for transfers between devices  282 us (57%)
  local copies, waits for them, and re-layouts  111 us (22%)
  starting transfers between devices  42.7 us (9%)
  other arithmetic  24.5 us (5%)
  matrix products  22.2 us (4%)
  between operations  14.5 us (3%)
    ppermute x10, waiting for transfers between devices, from_behind(): lax.ppermute(value, axis, [(source, source + steps) for source in range(f...  230 us
    unnamed x54, local copies, waits for them, and re-layouts  40.7 us
    ppermute x10, starting transfers between devices, from_behind(): lax.ppermute(value, axis, [(source, source + steps) for source in range(f...  34.8 us
    all_to_all x1, waiting for transfers between devices, shards(): lax.all_to_all(input_grad.astype(jnp.bfloat16), 'tp', split_axis=0, conca...  24.6 us
    another operation x3, local copies, waits for them, and re-layouts, shards(): jnp.stack([key_part.reshape(reach, tokens, width), value_part.reshape(rea...  22 us
    all_to_all x1, waiting for transfers between devices, shards(): local = lax.all_to_all(qkv, 'tp', split_axis=2, concat_axis=0, tiled=True)  19.9 us
    all_to_all x1, local copies, waits for them, and re-layouts, shards(): local = lax.all_to_all(qkv, 'tp', split_axis=2, concat_axis=0, tiled=True)  10.5 us
    slice x2, local copies, waits for them, and re-layouts, shards(): keys = joined[:, 0].reshape(reach * tokens, heads, HEAD_DIM)  10.1 us
  transfers between devices with their start and end apart: 13, of which 13 were waited for; matrix products, arithmetic and copies ran while one was open for 8% of the time, Pallas kernels for 0%

profile of v1, /device:TPU:0, one launch (start us, length us, event | category | flops | bytes accessed | tf_op | source)
XLA Modules:
  0.0 496.3 jit_solution(9346955197506745826)
XLA Ops:
  7.2 10.7 %copy.55 = bf16[32,3,8192]{0,1,2:T(4,128)(2,1)} copy(bf16[32,3,8192]{2,0,1:T(8,128)(2,1)} %param.4) | data formatting | bytes 3145728 | tf_op args[0]
  17.8 8.4 %reshape.159 = bf16[4,2,98304]{2,1,0:T(2,128)(2,1)} reshape(bf16[8192,3,32]{2,1,0:T(4,128)(2,1)} %bitcast.101) | data formatting | bytes 3145728
  26.2 4.3 all-to-all-start
  30.7 19.9 %all-to-all-done = bf16[4,2,98304]{2,1,0:T(2,128)(2,1)S(1)} async-done(((bf16[4,2,98304]{2,1,0:T(2,128)(2,1)}), bf16[4,2,98304]{2,1,0:T(2,128)(2,1)S(1)}, u32[]{:S(2)}, u32[]{:S(2)}) %all-to-all-start) | async-done | bytes 1572896 | tf_op jit(solution)/shard_map/all_to_all | solution.py:25
  50.6 7.1 %reshape.160 = bf16[8192,3,32]{2,1,0:T(4,128)(2,1)} reshape(bf16[4,2,98304]{2,1,0:T(2,128)(2,1)S(1)} %all-to-all-done) | data formatting | bytes 3145728
  57.7 10.5 %copy.57 = bf16[4,32,3,2048]{3,1,0,2:T(8,128)(2,1)S(1)} copy(bf16[4,32,3,2048]{1,2,3,0:T(4,128)(2,1)} %bitcast.100) | data formatting | bytes 3145728 | tf_op jit(solution)/shard_map/all_to_all | solution.py:25
  68.3 4.2 collective-permute-start
  81.5 5.3 %collective-permute-start.1 = (bf16[128,2,2048]{2,0,1:T(8,128)(2,1)S(1)}, bf16[128,2,2048]{2,0,1:T(8,128)(2,1)}, u32[]{:S(2)}, u32[]{:S(2)}) collective-permute-start(bf16[128,2,2048]{2,0,1:T(8,128)(2,1)S(1)} %get-tuple-element.24), channel_id=1, source_target_pairs={{0,4},{4,8},{8,12},{12,16},{16,20},{20,24},{24,28},{1,5},{5,9},{9,... | collective-permute-start | bytes 3145736 | tf_op jit(solution)/shard_map/ppermute | solution.py:15
  86.9 20.0 %collective-permute-done.1 = bf16[128,2,2048]{2,0,1:T(8,128)(2,1)} collective-permute-done((bf16[128,2,2048]{2,0,1:T(8,128)(2,1)S(1)}, bf16[128,2,2048]{2,0,1:T(8,128)(2,1)}, u32[]{:S(2)}, u32[]{:S(2)}) %collective-permute-start.1) | collective-permute-done | bytes 1048608 | tf_op jit(solution)/shard_map/ppermute | solution.py:15
  106.9 5.5 %collective-permute-start.2 = (bf16[128,2,2048]{2,0,1:T(8,128)(2,1)}, bf16[128,2,2048]{2,0,1:T(8,128)(2,1)}, u32[]{:S(2)}, u32[]{:S(2)}) collective-permute-start(bf16[128,2,2048]{2,0,1:T(8,128)(2,1)} %collective-permute-done.1), channel_id=1, source_target_pairs={{0,4},{4,8},{8,12},{12,16},{16,20},{20,24},{24,28},{1,5},{5,9},{9,... | collective-permute-start | bytes 3145736 | tf_op jit(solution)/shard_map/ppermute | solution.py:15
  112.9 18.9 %collective-permute-done.2 = bf16[128,2,2048]{2,0,1:T(8,128)(2,1)} collective-permute-done((bf16[128,2,2048]{2,0,1:T(8,128)(2,1)}, bf16[128,2,2048]{2,0,1:T(8,128)(2,1)}, u32[]{:S(2)}, u32[]{:S(2)}) %collective-permute-start.2) | collective-permute-done | bytes 1048608 | tf_op jit(solution)/shard_map/ppermute | solution.py:15
  131.8 6.2 %collective-permute-start.3 = (bf16[128,2,2048]{2,0,1:T(8,128)(2,1)}, bf16[128,2,2048]{2,0,1:T(8,128)(2,1)}, u32[]{:S(2)}, u32[]{:S(2)}) collective-permute-start(bf16[128,2,2048]{2,0,1:T(8,128)(2,1)} %collective-permute-done.2), channel_id=1, source_target_pairs={{0,4},{4,8},{8,12},{12,16},{16,20},{20,24},{24,28},{1,5},{5,9},{9,... | collective-permute-start | bytes 3145736 | tf_op jit(solution)/shard_map/ppermute | solution.py:15
  141.8 14.8 %collective-permute-done.3 = bf16[128,2,2048]{2,0,1:T(8,128)(2,1)} collective-permute-done((bf16[128,2,2048]{2,0,1:T(8,128)(2,1)}, bf16[128,2,2048]{2,0,1:T(8,128)(2,1)}, u32[]{:S(2)}, u32[]{:S(2)}) %collective-permute-start.3) | collective-permute-done | bytes 1048608 | tf_op jit(solution)/shard_map/ppermute | solution.py:15
  156.5 6.3 %collective-permute-start.4 = (bf16[128,2,2048]{2,0,1:T(8,128)(2,1)}, bf16[128,2,2048]{2,0,1:T(8,128)(2,1)}, u32[]{:S(2)}, u32[]{:S(2)}) collective-permute-start(bf16[128,2,2048]{2,0,1:T(8,128)(2,1)} %collective-permute-done.3), channel_id=1, source_target_pairs={{0,4},{4,8},{8,12},{12,16},{16,20},{20,24},{24,28},{1,5},{5,9},{9,... | collective-permute-start | bytes 3145736 | tf_op jit(solution)/shard_map/ppermute | solution.py:15
  182.7 5.7 %fusion.48 = (bf16[640,1,2048]{2,0,1:T(8,128)(2,1)}, bf16[640,1,2048]{2,0,1:T(8,128)(2,1)}) fusion(bf16[640,2,2048]{2,0,1:T(8,128)(2,1)} %constant_dynamic-update-slice_fusion), kind=kLoop, calls=%fused_computation.99 | loop fusion | bytes 10485760 | tf_op jit(solution)/shard_map/slice | solution.py:47
  188.4 4.4 copy.60
  192.8 4.5 copy.58
  197.2 6.6 %fusion.52 = (f32[16,128]{1,0:T(8,128)S(1)}, f32[16,128,640]{2,1,0:T(8,128)}) fusion(pred[128,640]{1,0:T(8,128)(4,1)} %and_and_fusion, bf16[128,16,128]{0,2,1:T(8,128)(2,1)} %bitcast.111, bf16[640,16,128]{0,2,1:T(8,128)(2,1)} %bitcast.102), kind=kOutput, calls=%fused_computation.103 | convolution fusion | flops 342098560 | bytes 8478720 | tf_op jit(solution)/shard_map/sub | solution.py:71
  203.8 4.1 fusion.18
  213.3 5.3 %copy.70 = f32[640,16,128]{2,1,0:T(8,128)} copy(f32[640,16,128]{2,0,1:T(8,128)S(1)} %fusion.18) | data formatting | bytes 10485760 | tf_op jit(solution)/shard_map/hqk,qhd->khd/transpose | solution.py:80
  218.7 6.8 %stack_reshape.7 = f32[5,128,1,2048]{3,1,0,2:T(8,128)} reshape(f32[640,16,128]{2,1,0:T(8,128)} %copy.70) | data formatting | bytes 10485760 | tf_op jit(solution)/shard_map/stack;reshape | solution.py:95
  225.5 5.0 %convolution_bitcast_fusion = f32[640,16,128]{0,2,1:T(8,128)} fusion(bf16[128,16,128]{0,2,1:T(8,128)(2,1)} %bitcast.112, bf16[16,128,640]{2,1,0:T(8,128)(2,1)} %fusion.2), kind=kOutput, calls=%fused_computation.48 | convolution fusion | flops 335544320 | bytes 8388608 | tf_op jit(solution)/shard_map/hqk,qhd->khd/dot_general | solution.py:92
  230.5 7.4 %reshape.153 = f32[5,128,1,2048]{1,0,3,2:T(8,128)} reshape(f32[640,16,128]{0,2,1:T(8,128)} %convolution_bitcast_fusion) | data formatting | bytes 10485760 | tf_op jit(solution)/shard_map/stack;reshape | solution.py:95
  237.8 7.8 %copy.71 = f32[5,128,1,2048]{3,1,2,0:T(8,128)} copy(f32[5,128,1,2048]{1,0,3,2:T(8,128)} %reshape.153) | data formatting | bytes 10485760 | tf_op jit(solution)/shard_map/stack;reshape | solution.py:95
  249.1 44.7 %collective-permute-done.5 = f32[128,2,2048]{2,0,1:T(8,128)S(1)} collective-permute-done((f32[128,2,2048]{2,0,1:T(8,128)S(1)}, f32[128,2,2048]{2,0,1:T(8,128)S(1)}, u32[]{:S(2)}, u32[]{:S(2)}) %collective-permute-start.5) | collective-permute-done | bytes 2097184 | tf_op jit(solution)/shard_map/ppermute | solution.py:15
  295.6 44.1 %collective-permute-done.6 = f32[128,2,2048]{2,0,1:T(8,128)S(1)} collective-permute-done((f32[128,2,2048]{2,0,1:T(8,128)S(1)}, f32[128,2,2048]{2,0,1:T(8,128)S(1)}, u32[]{:S(2)}, u32[]{:S(2)}) %collective-permute-start.6) | collective-permute-done | bytes 2097184 | tf_op jit(solution)/shard_map/ppermute | solution.py:15
  341.7 42.9 %collective-permute-done.7 = f32[128,2,2048]{2,0,1:T(8,128)S(1)} collective-permute-done((f32[128,2,2048]{2,0,1:T(8,128)S(1)}, f32[128,2,2048]{2,0,1:T(8,128)S(1)}, u32[]{:S(2)}, u32[]{:S(2)}) %collective-permute-start.7) | collective-permute-done | bytes 2097184 | tf_op jit(solution)/shard_map/ppermute | solution.py:15
  392.0 37.3 %collective-permute-done.8 = f32[128,2,2048]{2,0,1:T(8,128)} collective-permute-done((f32[128,2,2048]{2,0,1:T(8,128)}, f32[128,2,2048]{2,0,1:T(8,128)}, u32[]{:S(2)}, u32[]{:S(2)}) %collective-permute-start.8) | collective-permute-done | bytes 2097184 | tf_op jit(solution)/shard_map/ppermute | solution.py:15
  438.1 3.1 collective-permute-done.9
  448.8 3.6 all-to-all-start.1
  453.4 24.6 %all-to-all-done.1 = bf16[128,3,2048]{2,1,0:T(4,128)(2,1)S(1)} async-done(((bf16[128,3,2048]{2,1,0:T(4,128)(2,1)}), bf16[128,3,2048]{2,1,0:T(4,128)(2,1)S(1)}, u32[]{:S(2)}, u32[]{:S(2)}) %all-to-all-start.1) | async-done | bytes 1572896 | tf_op jit(solution)/shard_map/all_to_all | solution.py:115
  480.5 6.8 %all-gather.3.cloned.1.call-done = f32[24,7,2048]{2,1,0:T(8,128)} async-done(((f32[3,7,2048]{2,1,0:T(8,128)}), f32[24,7,2048]{2,1,0:T(8,128)}) %all-gather.3.cloned.1.call-update) | async-done | bytes 1376272 | tf_op jit(solution)/shard_map/all_gather | solution.py:114
  (106 shorter events, 75.0 us)
Async XLA Ops:
  26.2 4.3 copy-start.15
  26.2 24.4 %all-to-all-start = ((bf16[4,2,98304]{2,1,0:T(2,128)(2,1)}), bf16[4,2,98304]{2,1,0:T(2,128)(2,1)S(1)}, u32[]{:S(2)}, u32[]{:S(2)}) async-start(bf16[4,2,98304]{2,1,0:T(2,128)(2,1)} %reshape.159), calls=%async_computation | async-start | bytes 3145728 | tf_op jit(solution)/shard_map/all_to_all | solution.py:25
  30.5 456.7 %all-gather.3.cloned.1.call-start = ((), (), s32[]{:S(2)}) async-start(), calls=%async_computation.2 | async-start | bytes 1769472 | tf_op jit(solution)/shard_map/all_gather | solution.py:114
  68.2 4.3 copy-start.8
  68.3 6.4 %collective-permute-start = (bf16[6,3,2048]{2,0,1:T(8,128)(2,1)S(1)}, bf16[6,3,2048]{2,0,1:T(8,128)(2,1)S(1)}, u32[]{:S(2)}, u32[]{:S(2)}) collective-permute-start(bf16[6,3,2048]{2,0,1:T(8,128)(2,1)S(1)} %slice.138), channel_id=1, source_target_pairs={{0,4},{4,8},{8,12},{12,16},{16,20},{20,24},{24,28},{1,5},{5,9},{9,... | collective-permute-start | bytes 221192 | tf_op jit(solution)/shard_map/ppermute | solution.py:15
  72.5 6.7 %copy-start.13 = (f32[3,1,2048]{2,0,1:T(4,128)}, f32[3,1,2048]{2,0,1:T(4,128)S(1)}, u32[]{:S(2)}) copy-start(f32[3,1,2048]{2,0,1:T(4,128)S(1)} %copy.104) | copy-start | bytes 73732
  79.2 1.1 copy-start.9
  80.4 57.7 %copy-start.16 = (s32[8]{0:T(128)S(1)}, s32[8]{0:T(128)}, u32[]{:S(2)}) copy-start(s32[8]{0:T(128)} %param.6) | copy-start | bytes 100
  81.5 25.4 %collective-permute-start.1 = (bf16[128,2,2048]{2,0,1:T(8,128)(2,1)S(1)}, bf16[128,2,2048]{2,0,1:T(8,128)(2,1)}, u32[]{:S(2)}, u32[]{:S(2)}) collective-permute-start(bf16[128,2,2048]{2,0,1:T(8,128)(2,1)S(1)} %get-tuple-element.24), channel_id=1, source_target_pairs={{0,4},{4,8},{8,12},{12,16},{16,20},{20,24},{24,28},{1,5},{5,9},{9,... | collective-permute-start | bytes 3145736 | tf_op jit(solution)/shard_map/ppermute | solution.py:15
  106.9 24.9 %collective-permute-start.2 = (bf16[128,2,2048]{2,0,1:T(8,128)(2,1)}, bf16[128,2,2048]{2,0,1:T(8,128)(2,1)}, u32[]{:S(2)}, u32[]{:S(2)}) collective-permute-start(bf16[128,2,2048]{2,0,1:T(8,128)(2,1)} %collective-permute-done.1), channel_id=1, source_target_pairs={{0,4},{4,8},{8,12},{12,16},{16,20},{20,24},{24,28},{1,5},{5,9},{9,... | collective-permute-start | bytes 3145736 | tf_op jit(solution)/shard_map/ppermute | solution.py:15
  131.8 24.7 %collective-permute-start.3 = (bf16[128,2,2048]{2,0,1:T(8,128)(2,1)}, bf16[128,2,2048]{2,0,1:T(8,128)(2,1)}, u32[]{:S(2)}, u32[]{:S(2)}) collective-permute-start(bf16[128,2,2048]{2,0,1:T(8,128)(2,1)} %collective-permute-done.2), channel_id=1, source_target_pairs={{0,4},{4,8},{8,12},{12,16},{16,20},{20,24},{24,28},{1,5},{5,9},{9,... | collective-permute-start | bytes 3145736 | tf_op jit(solution)/shard_map/ppermute | solution.py:15
  156.5 23.9 %collective-permute-start.4 = (bf16[128,2,2048]{2,0,1:T(8,128)(2,1)}, bf16[128,2,2048]{2,0,1:T(8,128)(2,1)}, u32[]{:S(2)}, u32[]{:S(2)}) collective-permute-start(bf16[128,2,2048]{2,0,1:T(8,128)(2,1)} %collective-permute-done.3), channel_id=1, source_target_pairs={{0,4},{4,8},{8,12},{12,16},{16,20},{20,24},{24,28},{1,5},{5,9},{9,... | collective-permute-start | bytes 3145736 | tf_op jit(solution)/shard_map/ppermute | solution.py:15
  203.8 4.1 copy-start.7
  203.8 5.0 %copy-start.10 = (f32[16,128,640]{2,1,0:T(8,128)S(1)}, f32[16,128,640]{2,1,0:T(8,128)}, u32[]{:S(2)}) copy-start(f32[16,128,640]{2,1,0:T(8,128)} %get-tuple-element.39) | copy-start | bytes 15728644
  203.8 5.0 %copy-start.12 = (bf16[128,2048]{0,1:T(8,128)(2,1)S(1)}, bf16[128,2048]{0,1:T(8,128)(2,1)}, u32[]{:S(2)}) copy-start(bf16[128,2048]{0,1:T(8,128)(2,1)} %copy.63) | copy-start | bytes 1572868
  245.7 48.1 %slice-start = ((s8[5242880]{0:T(1024)(128)(4,1)}), s8[4194304]{0:T(1024)(128)(4,1)S(1)}, s32[]{:S(2)}) async-start(s8[5242880]{0:T(1024)(128)(4,1)} %bitcast.95), calls=%async_computation.3 | async-start | bytes 8388608
  245.7 48.1 %slice-start.1 = ((s8[5242880]{0:T(1024)(128)(4,1)}), s8[1048576]{0:T(1024)(128)(4,1)S(1)}, s32[]{:S(2)}) async-start(s8[5242880]{0:T(1024)(128)(4,1)} %bitcast.95), calls=%async_computation.4 | async-start | bytes 2097152
  245.7 48.1 %copy-start = (f32[5,128,1,2048]{3,1,2,0:T(8,128)S(1)}, f32[5,128,1,2048]{3,1,2,0:T(8,128)}, u32[]{:S(2)}) copy-start(f32[5,128,1,2048]{3,1,2,0:T(8,128)} %copy.71) | copy-start | bytes 15728644
  247.5 46.3 %collective-permute-start.5 = (f32[128,2,2048]{2,0,1:T(8,128)S(1)}, f32[128,2,2048]{2,0,1:T(8,128)S(1)}, u32[]{:S(2)}, u32[]{:S(2)}) collective-permute-start(f32[128,2,2048]{2,0,1:T(8,128)S(1)} %fusion.25), channel_id=1, source_target_pairs={{4,0},{8,4},{12,8},{16,12},{20,16},{24,20},{28,24},{5,1},{9,5},{13... | collective-permute-start | bytes 6291464 | tf_op jit(solution)/shard_map/ppermute | solution.py:15
  294.1 45.6 %collective-permute-start.6 = (f32[128,2,2048]{2,0,1:T(8,128)S(1)}, f32[128,2,2048]{2,0,1:T(8,128)S(1)}, u32[]{:S(2)}, u32[]{:S(2)}) collective-permute-start(f32[128,2,2048]{2,0,1:T(8,128)S(1)} %fusion.28), channel_id=1, source_target_pairs={{4,0},{8,4},{12,8},{16,12},{20,16},{24,20},{28,24},{5,1},{9,5},{13... | collective-permute-start | bytes 6291464 | tf_op jit(solution)/shard_map/ppermute | solution.py:15
  340.1 47.3 %copy-start.5 = (bf16[640,1,2048]{0,2,1:T(8,128)(2,1)S(1)}, bf16[640,1,2048]{0,2,1:T(8,128)(2,1)}, u32[]{:S(2)}) copy-start(bf16[640,1,2048]{0,2,1:T(8,128)(2,1)} %copy.60) | copy-start | bytes 7864324
  340.1 47.3 %copy-start.6 = (bf16[16,128,640]{2,1,0:T(8,128)(2,1)S(1)}, bf16[16,128,640]{2,1,0:T(8,128)(2,1)}, u32[]{:S(2)}) copy-start(bf16[16,128,640]{2,1,0:T(8,128)(2,1)} %fusion.2) | copy-start | bytes 7864324
  340.1 44.4 %collective-permute-start.7 = (f32[128,2,2048]{2,0,1:T(8,128)S(1)}, f32[128,2,2048]{2,0,1:T(8,128)S(1)}, u32[]{:S(2)}, u32[]{:S(2)}) collective-permute-start(f32[128,2,2048]{2,0,1:T(8,128)S(1)} %fusion.31), channel_id=1, source_target_pairs={{4,0},{8,4},{12,8},{16,12},{20,16},{24,20},{28,24},{5,1},{9,5},{13... | collective-permute-start | bytes 6291464 | tf_op jit(solution)/shard_map/ppermute | solution.py:15
  386.1 43.2 %collective-permute-start.8 = (f32[128,2,2048]{2,0,1:T(8,128)}, f32[128,2,2048]{2,0,1:T(8,128)}, u32[]{:S(2)}, u32[]{:S(2)}) collective-permute-start(f32[128,2,2048]{2,0,1:T(8,128)} %fusion.23), channel_id=1, source_target_pairs={{4,0},{8,4},{12,8},{16,12},{20,16},{24,20},{28,24},{5,1},{9,5},{13... | collective-permute-start | bytes 6291464 | tf_op jit(solution)/shard_map/ppermute | solution.py:15
  392.0 39.8 %copy-start.3 = (f32[128,1,2048]{2,0,1:T(8,128)S(1)}, f32[128,1,2048]{2,0,1:T(8,128)}, u32[]{:S(2)}) copy-start(f32[128,1,2048]{2,0,1:T(8,128)} %copy.73) | copy-start | bytes 3145732
  431.8 5.1 %copy-start.1 = (f32[128,2,2048]{2,0,1:T(8,128)}, f32[128,2,2048]{2,0,1:T(8,128)S(1)}, u32[]{:S(2)}) copy-start(f32[128,2,2048]{2,0,1:T(8,128)S(1)} %fusion.33) | copy-start | bytes 6291460
  432.6 8.6 %collective-permute-start.9 = (f32[6,3,2048]{2,0,1:T(8,128)}, f32[6,3,2048]{2,0,1:T(8,128)}, u32[]{:S(2)}, u32[]{:S(2)}) collective-permute-start(f32[6,3,2048]{2,0,1:T(8,128)} %fusion.45), channel_id=1, source_target_pairs={{4,0},{8,4},{12,8},{16,12},{20,16},{24,20},{28,24},{5,1},{9,5},{13... | collective-permute-start | bytes 442376 | tf_op jit(solution)/shard_map/ppermute | solution.py:15
  438.1 5.4 %copy-start.2 = (f32[128,2,2048]{2,0,1:T(8,128)S(1)}, f32[128,2,2048]{2,0,1:T(8,128)}, u32[]{:S(2)}) copy-start(f32[128,2,2048]{2,0,1:T(8,128)} %copy-done.1) | copy-start | bytes 6291460
  438.1 5.4 %copy-start.4 = (f32[128,1,2048]{2,0,1:T(8,128)S(1)}, f32[128,1,2048]{2,0,1:T(8,128)}, u32[]{:S(2)}) copy-start(f32[128,1,2048]{2,0,1:T(8,128)} %copy.73) | copy-start | bytes 3145732
  438.1 5.4 %copy-start.14 = (f32[3,1,2048]{2,0,1:T(4,128)S(1)}, f32[3,1,2048]{2,0,1:T(4,128)}, u32[]{:S(2)}) copy-start(f32[3,1,2048]{2,0,1:T(4,128)} %copy-done.13) | copy-start | bytes 73732
  446.1 6.3 %copy-start.11 = (bf16[128,16,128]{0,2,1:T(8,128)(2,1)S(1)}, bf16[128,16,128]{0,2,1:T(8,128)(2,1)}, u32[]{:S(2)}) copy-start(bf16[128,16,128]{0,2,1:T(8,128)(2,1)} %get-tuple-element.41) | copy-start | bytes 1572868
  448.8 29.3 %all-to-all-start.1 = ((bf16[128,3,2048]{2,1,0:T(4,128)(2,1)}), bf16[128,3,2048]{2,1,0:T(4,128)(2,1)S(1)}, u32[]{:S(2)}, u32[]{:S(2)}) async-start(bf16[128,3,2048]{2,1,0:T(4,128)(2,1)} %copy.74), calls=%async_computation.1 | async-start | bytes 4194304 | tf_op jit(solution)/shard_map/all_to_all | solution.py:115
Sparse Core Ops, SparseCore 0:
  438.2 49.0 all-gather.2
